TPU v7x, 32 devices: a whole 2x2x4 slice. The times are simulated.
32 devices in a mesh: aux: 16 (over z, y, x), grp: 2 (over core).
Axes of the slice: x: 2, y: 2, z: 4, core: 2. Of those that a mesh axis runs over, the one named last changes fastest.
Arguments:
- integrals: bfloat16 [1024, 16, 4096], P(('aux', 'grp')), may hold values from -6 to 6
- block_pairs: int32 [32, 16, 2], P(('aux', 'grp')), may hold values from 0 to 63
- occupied: bfloat16 [2, 4096], replicated, may hold values from -0.75 to 0.75
- virtual: bfloat16 [4096, 3072], P(None, 'grp'), may hold values from -0.1875 to 0.1875
- stored: bfloat16 [1024, 6144], P('aux'), may hold values from -0.1875 to 0.1875
Outputs:
- exchange_panel: bfloat16 [2, 3072, 2, 3072], P(None, ('grp', 'aux'))
Inputs may be any that keep to these rules, and one draw needn't show every extreme that they name: `block_pairs`: block pairs may repeat within a shard; repeated blocks add.
All inputs are finite; a program needn't handle non-finite values.
Results may differ from a plain program's by a relative error of at most 0.0095.
Values may be sent and summed in bfloat16 or wider, within the bound.
A program may use at most 192 MiB of HBM per device.

v0:
```python
import functools
import math

import jax
import jax.numpy as jnp
from jax import lax
from jax.experimental import pallas as pl
from jax.experimental.pallas import tpu as pltpu
from jax.sharding import PartitionSpec as P

MESH = pl.DeviceIdType.MESH
LANES = 128
PLANE = 4
PIECES = 3
FIRST = 1


def spans_of(width):
    piece = width // PIECES // LANES * LANES
    starts = [n * piece for n in range(PIECES)] + [width]
    return [(a, b - a, 0 if n < FIRST else 1) for n, (a, b) in enumerate(zip(starts, starts[1:]))]


def weigh(pairs, occ, weights):
    nb = pairs.shape[0]
    nocc, nblocks, blk = occ.shape
    lanes = lax.broadcasted_iota(jnp.int32, (nb, nblocks), 1)
    pick = (pairs[:, 0:1] == lanes).astype(jnp.bfloat16)
    step = 8 * LANES
    row = lax.broadcasted_iota(jnp.int32, (blk, step), 0) * blk
    col = lax.broadcasted_iota(jnp.int32, (blk, step), 1)
    for i in range(nocc):
        picked = jnp.dot(pick, occ[i], preferred_element_type=jnp.float32).astype(jnp.bfloat16)
        for t in range(weights.shape[2] // step):
            offset = col + t * step - row
            spread = ((offset >= 0) & (offset < blk)).astype(jnp.bfloat16)
            weights[i, :, t * step:(t + 1) * step] = jnp.dot(
                picked, spread, preferred_element_type=jnp.float32)


def contract(blk, integrals, weights, part):
    aux_rows = integrals.shape[0]
    nocc = weights.shape[0]

    @pl.loop(0, aux_rows)
    def _(p):
        for i in range(nocc):
            sums = [None, None]
            for t in range(integrals.shape[2] // LANES):
                cols = slice(t * LANES, (t + 1) * LANES)
                term = integrals[p, :, cols].astype(jnp.float32) * weights[i, :, cols]
                sums[t % 2] = term if sums[t % 2] is None else sums[t % 2] + term
            total = sums[0] + sums[1]
            whole = total
            for f in range(1, LANES // blk):
                whole = whole + pltpu.roll(total, f * blk, 1)
            part[i * aux_rows + p] = whole


def place(blk, pairs, part, turned, half, grp):
    nb = pairs.shape[0]
    per = LANES // blk
    for k in range(nb):
        turned[k] = part[:, k, :]
    lane = lax.broadcasted_iota(jnp.int32, (1, LANES), 1) // blk

    @pl.loop(0, half.shape[2] // LANES)
    def _(b):
        here = lane + b * per
        total = None
        for k in range(nb):
            term = jnp.where(here == pairs[k:k + 1, 1:2], turned[k], 0.0)
            total = term if total is None else total + term
        half[grp, :, pl.ds(pl.multiple_of(b * LANES, LANES), LANES)] = total.astype(half.dtype)


def multiply(nocc, local, half, virt, chunk):
    n_grp, both, nbas = half.shape
    aux_rows = both // nocc
    step = math.lcm(local, LANES)
    for t in range(virt.shape[1] // step):
        product = jnp.dot(
            half[...].reshape(n_grp * both, nbas), virt[:, t * step:(t + 1) * step],
            preferred_element_type=jnp.float32)
        for c in range(step // local):
            d = t * (step // local) + c
            for q in range(n_grp):
                for i in range(nocc):
                    top = q * both + i * aux_rows
                    chunk[d, q * aux_rows:(q + 1) * aux_rows, i * local:(i + 1) * local] = product[
                        top:top + aux_rows, c * local:(c + 1) * local].astype(chunk.dtype)


def panel_kernel(n_aux, n_grp, integrals, pairs_in, occ, virtual, stored, out, rows, fac, total, block,
                 ints, virt, weights, part, turned, half, chunk,
                 own_sem, recv, send, frecv, fsend, precv, psend, orecv, osend, hrecv, hsend):
    me = lax.axis_index("aux")
    grp = lax.axis_index("grp")
    line = n_aux // PLANE
    width = rows.shape[2]
    spans = spans_of(width)
    z = me // PLANE
    su = 1 + grp % 2
    sv = 3 - su
    u = (me // su) % 2
    v = (me // sv) % 2
    next_u = me + su * (1 - 2 * u)
    next_v = me + sv * (1 - 2 * v)
    up, down = z + 1 < line, z >= 1
    targets = {"up": me + PLANE, "down": me - PLANE, "u": next_u, "v": next_v}
    slots = {"up": 0, "down": 1, "u": 2, "v": 3}

    load = pltpu.make_async_copy(
        stored.at[:, pl.ds(pl.multiple_of(grp * width, LANES), width)], rows.at[me], own_sem.at[0])
    load.start()
    mine = pltpu.make_async_copy(chunk.at[me], fac.at[grp, me], own_sem.at[1])
    load_ints = pltpu.make_async_copy(integrals, ints, own_sem.at[3])
    load_ints.start()
    load_virt = pltpu.make_async_copy(virtual, virt, own_sem.at[4])
    load_virt.start()
    pairs = pairs_in.at[0]
    nocc, nblocks, blk = occ.shape
    local = virtual.shape[1] // n_aux

    barrier = pltpu.get_barrier_semaphore()
    for o in range(1, n_aux):
        pl.semaphore_signal(barrier, inc=1, device_id=(lax.rem(me + o, n_aux), grp), device_id_type=MESH)
    for o in range(1, n_grp):
        pl.semaphore_signal(barrier, inc=1, device_id=(me, lax.rem(grp + o, n_grp)), device_id_type=MESH)
    pl.semaphore_wait(barrier, n_aux - 1 + n_grp - 1)

    def copy(source, colour, way):
        at = rows.at[source, :, pl.ds(*spans[colour][:2])]
        return pltpu.make_async_remote_copy(
            src_ref=at, dst_ref=at,
            send_sem=send.at[colour, slots[way], source], recv_sem=recv.at[colour, source],
            device_id=(targets[way], grp), device_id_type=MESH)

    def when(condition, action):
        if condition is None:
            action()
        else:
            pl.when(condition)(action)

    edges = {"up": up, "down": down, "u": None, "v": None}

    def ways_of(dz, du, dv, colour):
        if dv:
            return ()
        along = ("up", "down") if dz == 0 else (("up",) if dz > 0 else ("down",))
        if colour == 0:
            return ("v",) if du else along + ("u", "v")
        if dz == 0 and du == 0:
            return ("u",) + along + ("v",)
        return along + ("v",)

    def source_of(dz, du, dv):
        return (z - dz) * PLANE + su * (u + du * (1 - 2 * u)) + sv * (v + dv * (1 - 2 * v))

    def valid(dz):
        if dz == 0:
            return None
        return z - dz >= 0 if dz > 0 else z - dz < line

    sent = []

    def forward(dz, du, dv):
        source = source_of(dz, du, dv)
        for colour in range(len(spans)):
            ways = ways_of(dz, du, dv, spans[colour][2])
            sent.append((dz, source, colour, ways))

            def act(colour=colour, ways=ways):
                if (dz, du, dv) != (0, 0, 0):
                    copy(source, colour, "v").wait_recv()
                for way in ways:
                    when(edges[way], copy(source, colour, way).start)

            when(valid(dz), act)

    def plane_dot(dz, first):
        def act():
            base = (z - dz) * PLANE
            tile = 512 if width % 512 == 0 else LANES

            @pl.loop(0, width // tile)
            def _(t):
                cols = pl.ds(pl.multiple_of(t * tile, tile), tile)
                right = rows[pl.ds(base, PLANE), :, cols].reshape(-1, tile)
                for q in range(n_grp):
                    left = fac[q, pl.ds(base, PLANE)].reshape(-1, fac.shape[3])
                    term = lax.dot_general(
                        left, right, (((0,), (0,)), ((), ())), preferred_element_type=jnp.float32)
                    if first:
                        total[q, :, cols] = term
                    else:
                        total[q, :, cols] += term

        when(valid(dz), act)

    offsets = [(dz, du, dv) for dz in range(1 - line, line) for du in (0, 1) for dv in (0, 1)]
    hops = lambda o: abs(o[0]) + o[1] + o[2]
    last_hop = line + 1

    def fac_copy(o):
        to = lax.rem(me + o, n_aux)
        return pltpu.make_async_remote_copy(
            src_ref=chunk.at[to], dst_ref=fac.at[grp, me], send_sem=fsend.at[o], recv_sem=frecv.at[o],
            device_id=(to, grp), device_id_type=MESH)

    def fac_wait(o):
        source = lax.rem(me + n_aux - o, n_aux)
        pltpu.make_async_remote_copy(
            src_ref=chunk.at[0], dst_ref=fac.at[grp, source], send_sem=fsend.at[o], recv_sem=frecv.at[o],
            device_id=(source, grp), device_id_type=MESH).wait_recv()
        return source

    def share(o, source, p):
        return pltpu.make_async_remote_copy(
            src_ref=fac.at[grp, source], dst_ref=fac.at[grp, source],
            send_sem=psend.at[p, o], recv_sem=precv.at[p, o],
            device_id=(me, lax.rem(grp + p, n_grp)), device_id_type=MESH)

    def half_copy(p):
        return pltpu.make_async_remote_copy(
            src_ref=half.at[grp], dst_ref=half.at[grp], send_sem=hsend.at[p], recv_sem=hrecv.at[p],
            device_id=(me, lax.rem(grp + p, n_grp)), device_id_type=MESH)

    for hop in range(last_hop + 1):
        if hop == 0:
            load.wait()
        for offset in offsets:
            if hops(offset) == hop:
                forward(*offset)
        if hop == 0:
            weigh(pairs, occ, weights)
            load_ints.wait()
            contract(blk, ints, weights, part)
            place(blk, pairs, part, turned, half, grp)
            for p in range(1, n_grp):
                half_copy(p).start()
        if hop == 1:
            for p in range(1, n_grp):
                giver = lax.rem(grp + n_grp - p, n_grp)
                pltpu.make_async_remote_copy(
                    src_ref=half.at[giver], dst_ref=half.at[giver], send_sem=hsend.at[p],
                    recv_sem=hrecv.at[p], device_id=(me, giver), device_id_type=MESH).wait_recv()
            load_virt.wait()
            multiply(nocc, local, half, virt, chunk)
            mine.start()
            for o in range(1, n_aux):
                fac_copy(o).start()
            mine.wait()
        if hop == 2:
            for o in range(n_aux):
                source = me if o == 0 else fac_wait(o)
                for p in range(1, n_grp):
                    share(o, source, p).start()
            for o in range(n_aux):
                source = lax.rem(me + n_aux - o, n_aux)
                for p in range(1, n_grp):
                    giver = lax.rem(grp + n_grp - p, n_grp)
                    pltpu.make_async_remote_copy(
                        src_ref=fac.at[grp, source], dst_ref=fac.at[giver, source],
                        send_sem=psend.at[p, o], recv_sem=precv.at[p, o],
                        device_id=(me, giver), device_id_type=MESH).wait_recv()
        if hop >= 2:
            for dz in sorted({hop - 2, 2 - hop}):
                plane_dot(dz, hop == 2)

    def give(p, n):
        to = lax.rem(grp + p, n_grp)
        cols = pl.ds(*spans[n][:2])
        return pltpu.make_async_remote_copy(
            src_ref=block.at[to, :, cols], dst_ref=out.at[grp, :, cols],
            send_sem=osend.at[p, n], recv_sem=orecv.at[p, n],
            device_id=(me, to), device_id_type=MESH)

    for p in range(1, n_grp):
        to = lax.rem(grp + p, n_grp)
        for n in range(len(spans)):
            cols = pl.ds(*spans[n][:2])
            block[to, :, cols] = total[to, :, cols].astype(block.dtype)
            give(p, n).start()
    block[grp] = total[grp].astype(block.dtype)
    keep = pltpu.make_async_copy(block.at[grp], out.at[grp], own_sem.at[2])
    keep.start()

    for dz, source, colour, ways in sent:
        def drain(source=source, colour=colour, ways=ways):
            for way in ways:
                when(edges[way], copy(source, colour, way).wait_send)
        if ways:
            when(valid(dz), drain)
    for p in range(1, n_grp):
        half_copy(p).wait_send()
    for o in range(1, n_aux):
        fac_copy(o).wait_send()
    for o in range(n_aux):
        source = lax.rem(me + n_aux - o, n_aux)
        for p in range(1, n_grp):
            share(o, source, p).wait_send()
    for p in range(1, n_grp):
        giver = lax.rem(grp + n_grp - p, n_grp)
        for n in range(len(spans)):
            cols = pl.ds(*spans[n][:2])
            give(p, n).wait_send()
            pltpu.make_async_remote_copy(
                src_ref=block.at[giver, :, cols], dst_ref=out.at[giver, :, cols],
                send_sem=osend.at[p, n], recv_sem=orecv.at[p, n],
                device_id=(me, giver), device_id_type=MESH).wait_recv()
    keep.wait()


def panels(integrals, pairs, occ, virtual, stored, n_aux, n_grp):
    depth = stored.shape[0]
    width = stored.shape[1] // n_grp
    aux_rows, nb, flat = integrals.shape
    nocc, nblocks, blk = occ.shape
    nbas, slab = virtual.shape
    pieces = len(spans_of(width))
    cols = nocc * (slab // n_aux)
    dma = pltpu.SemaphoreType.DMA
    hbm = pl.BlockSpec(memory_space=pltpu.HBM)
    vmem = pl.BlockSpec(memory_space=pltpu.VMEM)
    return pl.pallas_call(
        functools.partial(panel_kernel, n_aux, n_grp),
        out_shape=jax.ShapeDtypeStruct((n_grp, cols, width), jnp.bfloat16),
        in_specs=[hbm, vmem, vmem, hbm, hbm],
        out_specs=hbm,
        scratch_shapes=[
            pltpu.VMEM((n_aux, depth, width), jnp.bfloat16),
            pltpu.VMEM((n_grp, n_aux, depth, cols), jnp.bfloat16),
            pltpu.VMEM((n_grp, cols, width), jnp.float32),
            pltpu.VMEM((n_grp, cols, width), jnp.bfloat16),
            pltpu.VMEM(integrals.shape, jnp.bfloat16),
            pltpu.VMEM(virtual.shape, jnp.bfloat16),
            pltpu.VMEM((nocc, nb, flat), jnp.float32),
            pltpu.VMEM((nocc * aux_rows, nb, LANES), jnp.float32),
            pltpu.VMEM((nb, nocc * aux_rows, LANES), jnp.float32),
            pltpu.VMEM((n_grp, nocc * aux_rows, nbas), jnp.bfloat16),
            pltpu.VMEM((n_aux, depth, cols), jnp.bfloat16),
            dma((5,)),
            dma((pieces, n_aux)),
            dma((pieces, 4, n_aux)),
            dma((n_aux,)),
            dma((n_aux,)),
            dma((n_grp, n_aux)),
            dma((n_grp, n_aux)),
            dma((n_grp, pieces)),
            dma((n_grp, pieces)),
            dma((n_grp,)),
            dma((n_grp,)),
        ],
        compiler_params=pltpu.CompilerParams(
            collective_id=0, has_side_effects=True, vmem_limit_bytes=63 * 1024 * 1024),
    )(integrals, pairs, occ, virtual, stored)


def make_per_device(n_aux, n_grp, v):
    def per_device(integrals, block_pairs, occupied, virtual, stored):
        nocc, nbas = occupied.shape
        local = virtual.shape[1] // n_aux
        blk = math.isqrt(integrals.shape[2])
        occ = occupied.reshape(nocc, nbas // blk, blk)
        panel = panels(integrals, block_pairs, occ, virtual, stored, n_aux, n_grp)
        return panel.transpose(1, 0, 2).reshape(nocc, local, n_grp * panel.shape[2] // v, v)

    return per_device


def solution(mesh):
    n_aux, n_grp = mesh.shape["aux"], mesh.shape["grp"]

    def whole(integrals, block_pairs, occupied, virtual, stored):
        return jax.shard_map(
            make_per_device(n_aux, n_grp, virtual.shape[1]),
            mesh=mesh,
            in_specs=(
                P(("aux", "grp"), None, None),
                P(("aux", "grp"), None, None),
                P(),
                P(None, "grp"),
                P("aux", None),
            ),
            out_specs=P(None, ("grp", "aux"), None, None),
            check_vma=False,
        )(integrals, block_pairs, occupied, virtual, stored)

    return whole
```

profile of v0, /device:TPU:5, one launch (start us, length us, event | category | flops | bytes accessed | tf_op | source)
XLA Modules:
  0.0 77.8 jit_solution(8712741726063751736)
XLA Ops:
  0.0 1.3 %copy.6.pairs_in = s32[1,16,2]{2,1,0:T(8,128)} copy(s32[1,16,2]{1,2,0:T(2,128)} %param.6) | data formatting | bytes 256 | tf_op args[1]
  1.3 1.4 %reshape.6.occ = bf16[2,64,64]{2,1,0:T(8,128)(2,1)} reshape(bf16[2,4096]{1,0:T(2,128)(2,1)} %param.7) | data formatting | bytes 32768 | tf_op jit(solution)/shard_map/reshape | solution.py:365
  2.8 69.5 %shard_map.55 = bf16[2,192,3072]{2,1,0:T(8,128)(2,1)} custom-call(bf16[32,16,4096]{2,1,0:T(8,128)(2,1)} %integrals.1, s32[1,16,2]{2,1,0:T(8,128)} %copy.6.pairs_in, bf16[2,64,64]{2,1,0:T(8,128)(2,1)} %reshape.6.occ, bf16[4096,1536]{1,0:T(8,128)(2,1)} %virtual.1, bf16[64,6144]{1,0:T(8,128)(2,1)} %stored.1), custom_call_target="tpu_custom_call" | custom-call | tf_op jit(solution)/shard_map/pallas_call | solution.py:326
  72.3 5.5 %copy.7 = bf16[2,96,2,3072]{3,2,1,0:T(2,128)(2,1)} copy(bf16[2,96,2,3072]{3,1,0,2:T(8,128)(2,1)} %bitcast.3) | data formatting | bytes 4718592 | tf_op jit(solution)/shard_map/reshape | solution.py:367
where the time goes:
time: 79.4 us; the launch traced here: 77.8 us
  Pallas kernels  69.5 us (88%)
  local copies, waits for them, and re-layouts  8.27 us (10%)
    pallas_call x1, Pallas kernels, panels(): pl.pallas_call(functools.partial(panel_kernel, n_aux, n_grp), out_shape=j...  69.5 us
    reshape x1, local copies, waits for them, and re-layouts, per_device(): panel.transpose(1, 0, 2)  5.5 us

commit v1 on v0

--- a/solution.py
+++ b/solution.py
@@ -91,7 +91,7 @@
                         top:top + aux_rows, c * local:(c + 1) * local].astype(chunk.dtype)
 
 
-def panel_kernel(n_aux, n_grp, integrals, pairs_in, occ, virtual, stored, out, rows, fac, total, block,
+def panel_any_kernel(n_aux, n_grp, integrals, pairs_in, occ, virtual, stored, out, rows, fac, total, block,
                  ints, virt, weights, part, turned, half, chunk,
                  own_sem, recv, send, frecv, fsend, precv, psend, orecv, osend, hrecv, hsend):
     me = lax.axis_index("aux")
@@ -312,7 +312,7 @@
     keep.wait()
 
 
-def panels(integrals, pairs, occ, virtual, stored, n_aux, n_grp):
+def panels_any(integrals, pairs, occ, virtual, stored, n_aux, n_grp):
     depth = stored.shape[0]
     width = stored.shape[1] // n_grp
     aux_rows, nb, flat = integrals.shape
@@ -324,7 +324,7 @@
     hbm = pl.BlockSpec(memory_space=pltpu.HBM)
     vmem = pl.BlockSpec(memory_space=pltpu.VMEM)
     return pl.pallas_call(
-        functools.partial(panel_kernel, n_aux, n_grp),
+        functools.partial(panel_any_kernel, n_aux, n_grp),
         out_shape=jax.ShapeDtypeStruct((n_grp, cols, width), jnp.bfloat16),
         in_specs=[hbm, vmem, vmem, hbm, hbm],
         out_specs=hbm,
@@ -357,13 +357,379 @@
     )(integrals, pairs, occ, virtual, stored)
 
 
+def weigh_blocks(pairs, occ, weights):
+    nocc, nbas = occ.shape
+    nb = pairs.shape[1]
+    blk = math.isqrt(weights.shape[2])
+    per = LANES // blk
+    tiles = nbas // LANES
+    line = lax.broadcasted_iota(jnp.int32, (tiles, nb), 0) * per
+    step = 8 * LANES
+    row = lax.broadcasted_iota(jnp.int32, (blk, step), 0) * blk
+    col = lax.broadcasted_iota(jnp.int32, (blk, step), 1)
+    orbital = occ[...].astype(jnp.float32)
+    for i in range(nocc):
+        table = jnp.concatenate(
+            [orbital[i:i + 1, t * LANES:(t + 1) * LANES] for t in range(tiles)], axis=0).astype(jnp.bfloat16)
+        picked = None
+        for f in range(per):
+            pick = (pairs[0:1, :] == line + f).astype(jnp.bfloat16)
+            term = lax.dot_general(
+                pick, table[:, f * blk:(f + 1) * blk], (((0,), (0,)), ((), ())), preferred_element_type=jnp.float32)
+            picked = term if picked is None else picked + term
+        picked = picked.astype(jnp.bfloat16)
+        for t in range(weights.shape[2] // step):
+            offset = col + t * step - row
+            spread = ((offset >= 0) & (offset < blk)).astype(jnp.bfloat16)
+            weights[i, :, t * step:(t + 1) * step] = jnp.dot(
+                picked, spread, preferred_element_type=jnp.float32)
+
+
+def compact(blk, part, half, grp):
+    nb = part.shape[1]
+    per = LANES // blk
+    lane = lax.broadcasted_iota(jnp.int32, (part.shape[0], LANES), 1) // blk
+    for t in range(nb // per):
+        tile = part[:, t * per, :]
+        for f in range(1, per):
+            tile = jnp.where(lane == f, part[:, t * per + f, :], tile)
+        half[grp, :, t * LANES:(t + 1) * LANES] = tile.astype(half.dtype)
+
+
+def expand(nocc, local, blk, index, half, virt, chunk):
+    n_grp, both, depth = half.shape
+    aux_rows = both // nocc
+    wide = 2 * local
+    step = math.lcm(wide, 2 * LANES)
+    for q in range(n_grp):
+        for t in range(virt.shape[2] // step):
+            cols = slice(t * step, (t + 1) * step)
+            right = jnp.concatenate([virt[index[q, 1, k], :, cols] for k in range(depth // blk)], axis=0)
+            product = jnp.dot(half[q], right, preferred_element_type=jnp.float32).astype(chunk.dtype)
+            for c in range(step // wide):
+                for i in range(nocc):
+                    chunk[t * (step // wide) + c, q * aux_rows:(q + 1) * aux_rows, i * wide:(i + 1) * wide] = product[
+                        i * aux_rows:(i + 1) * aux_rows, c * wide:(c + 1) * wide]
+
+
+def panel_kernel(n_aux, v, piece, integrals, pairs_in, occ_in, virtual, stored, out, rows, fac, turned, block,
+                 ints, virt, weights, part, half, chunk, pairs, index, occ,
+                 load_sem, own_sem, xsend, xrecv, send, recv, hsend, hrecv, fsend, frecv, gsend, grecv, psend, precv,
+                 osend, orecv):
+    me = lax.axis_index("aux")
+    grp = lax.axis_index("grp")
+    other = 1 - grp
+    line = n_aux // PLANE
+    nj = stored.shape[1] // v
+    quarter = v // 4
+    pieces = quarter // piece
+    nocc = occ.shape[0]
+    blk = math.isqrt(integrals.shape[2])
+    local = virtual.shape[2] // n_aux
+    z = me // PLANE
+    x = me % 2
+    y = (me // 2) % 2
+    pair = me // 2
+    n_pairs = n_aux // 2
+    xmate = me + 1 - 2 * x
+    ymate = me + 2 * (1 - 2 * y)
+    targets = {"up": me + PLANE, "down": me - PLANE, "y": ymate}
+    slots = {"up": 0, "down": 1, "y": 2}
+    edges = {"up": z + 1 < line, "down": z >= 1, "y": None}
+    mine = 2 * x + grp
+    theirs = 2 * (1 - x) + grp
+
+    def column(j, q, n):
+        return pl.ds(pl.multiple_of(j * v + q * quarter + n * piece, LANES), piece)
+
+    load_pairs = pltpu.make_async_copy(pairs_in.at[0], pairs.at[grp], load_sem.at[0])
+    load_pairs.start()
+    load_occ = pltpu.make_async_copy(occ_in, occ, load_sem.at[1])
+    load_occ.start()
+    load_ints = pltpu.make_async_copy(integrals, ints, load_sem.at[2])
+    load_ints.start()
+    for n in range(pieces):
+        for j in range(nj):
+            pltpu.make_async_copy(
+                stored.at[:, column(j, mine, n)], rows.at[n, me, :, pl.ds(j * piece, piece)], own_sem.at[n, j]).start()
+    load_virt = pltpu.make_async_copy(virtual, virt, load_sem.at[3])
+    load_virt.start()
+
+    barrier = pltpu.get_barrier_semaphore()
+    peers = [((pair + o) % n_pairs * 2 + x, grp) for o in range(1, n_pairs)]
+    peers += [(xmate, grp), (xmate, other), (me, other)]
+    for peer in peers:
+        pl.semaphore_signal(barrier, inc=1, device_id=peer, device_id_type=MESH)
+
+    def when(condition, action):
+        if condition is None:
+            action()
+        else:
+            pl.when(condition)(action)
+
+    def remote(src, dst, send_sem, recv_sem, device):
+        return pltpu.make_async_remote_copy(
+            src_ref=src, dst_ref=dst, send_sem=send_sem, recv_sem=recv_sem, device_id=device, device_id_type=MESH)
+
+    def copy(n, source, way):
+        at = rows.at[n, source]
+        return remote(at, at, send.at[n, slots[way], source], recv.at[n, source], (targets[way], grp))
+
+    def cross(n, j):
+        return remote(
+            stored.at[:, column(j, theirs, n)], rows.at[n, me, :, pl.ds(j * piece, piece)],
+            xsend.at[n, j], xrecv.at[n, j], (xmate, grp))
+
+    def cross_wait(n, j):
+        at = rows.at[n, xmate, :, pl.ds(j * piece, piece)]
+        remote(at, at, xsend.at[n, j], xrecv.at[n, j], (xmate, grp)).wait_recv()
+
+    def valid(dz):
+        if dz == 0:
+            return None
+        return z - dz >= 0 if dz > 0 else z - dz < line
+
+    sent = []
+
+    def forward(n, dz, far):
+        source = (z - dz) * PLANE + y * 2 + (1 - x if far else x)
+        ways = ("up", "down", "y") if dz == 0 else (("up", "y") if dz > 0 else ("down", "y"))
+        sent.append((n, dz, source, ways))
+
+        def act():
+            if dz == 0:
+                for j in range(nj):
+                    if far:
+                        cross_wait(n, j)
+                    else:
+                        at = rows.at[n, me, :, pl.ds(j * piece, piece)]
+                        pltpu.make_async_copy(stored.at[:, column(j, mine, n)], at, own_sem.at[n, j]).wait()
+            else:
+                copy(n, source, "y").wait_recv()
+            for way in ways:
+                when(edges[way], copy(n, source, way).start)
+
+        when(valid(dz), act)
+
+    def stage(group, distance, far):
+        for n in group:
+            for dz in sorted({distance, -distance}):
+                forward(n, dz, far)
+
+    def half_copy():
+        return remote(half.at[grp], half.at[grp], hsend.at[0], hrecv.at[0], (me, other))
+
+    def pairs_copy():
+        return remote(pairs.at[grp], pairs.at[grp], hsend.at[1], hrecv.at[1], (me, other))
+
+    def fac_copy(o):
+        to = (pair + o) % n_pairs
+        return remote(chunk.at[to], fac.at[grp, me], fsend.at[o], frecv.at[o], (to * 2 + x, grp))
+
+    def fac_source(o):
+        return (pair + n_pairs - o) % n_pairs * 2
+
+    def fac_cross(o):
+        source = fac_source(o) + x
+        return remote(fac.at[grp, source], fac.at[grp, source], gsend.at[o], grecv.at[o], (xmate, grp))
+
+    def share(o, far):
+        source = fac_source(o) + (1 - x if far else x)
+        return remote(
+            fac.at[grp, source], fac.at[grp, source], psend.at[int(far), o], precv.at[int(far), o], (me, other))
+
+    def give(n, rel, q, j):
+        to = (grp + q) % 2
+        chip = 1 - x if rel else x
+        at = xmate if rel else me
+        src = block.at[n, to, chip, :, pl.ds(j * piece, piece)]
+        dst = out.at[j, :, column(0, mine, n)]
+        if not rel and not q:
+            return pltpu.make_async_copy(src, dst, osend.at[n, 0, j])
+        return remote(src, dst, osend.at[n, 2 * rel + q, j], orecv.at[n, 2 * rel + q, j], (at, to))
+
+    def taken(n, rel, q, j):
+        source = 2 * (1 - x if rel else x) + (grp + q) % 2
+        dst = out.at[j, :, column(0, source, n)]
+        src = block.at[n, 0, 0, :, pl.ds(j * piece, piece)]
+        return remote(src, dst, osend.at[n, 2 * rel + q, j], orecv.at[n, 2 * rel + q, j], (xmate, grp))
+
+    def finish(n):
+        for dz in range(1 - line, line):
+            for far in (0, 1):
+                source = (z - dz) * PLANE + (1 - y) * 2 + far
+
+                def arrive(source=source):
+                    copy(n, source, "y").wait_recv()
+
+                when(valid(dz), arrive)
+        right = rows[n].reshape(-1, nj * piece)
+        for q in range(2):
+            term = jnp.dot(turned[q], right, preferred_element_type=jnp.float32).astype(block.dtype)
+            for i in range(nocc):
+                for chip in range(2):
+                    top = (i * 2 + chip) * local
+                    block[n, q, chip, i * local:(i + 1) * local] = term[top:top + local]
+        for rel, q in ((1, 0), (1, 1), (0, 1), (0, 0)):
+            for j in range(nj):
+                give(n, rel, q, j).start()
+
+    first = list(range((pieces + 1) // 2))
+    last = list(range((pieces + 1) // 2, pieces))
+    far_hops = range(2, line)
+
+    load_pairs.wait()
+    load_occ.wait()
+    weigh_blocks(pairs[grp], occ, weights)
+    load_ints.wait()
+    contract(blk, ints, weights, part)
+    pl.semaphore_wait(barrier, len(peers))
+    pairs_copy().start()
+    for n in range(pieces):
+        for j in range(nj):
+            cross(n, j).start()
+    stage(first, 0, False)
+    compact(blk, part, half, grp)
+    half_copy().start()
+    remote(pairs.at[other], pairs.at[other], hsend.at[1], hrecv.at[1], (me, other)).wait_recv()
+    load_index = pltpu.make_async_copy(pairs, index, load_sem.at[0])
+    load_index.start()
+    stage(first, 0, True)
+    load_index.wait()
+    load_virt.wait()
+    remote(half.at[other], half.at[other], hsend.at[0], hrecv.at[0], (me, other)).wait_recv()
+    expand(nocc, local, blk, index, half, virt, chunk)
+    for o in range(1, n_pairs):
+        fac_copy(o).start()
+    keep = pltpu.make_async_copy(chunk.at[pair], fac.at[grp, me], load_sem.at[1])
+    keep.start()
+    stage(first, 1, False)
+    stage(first, 1, True)
+    stage(last, 0, False)
+    keep.wait()
+    for o in range(n_pairs):
+        if o:
+            source = fac_source(o) + x
+            remote(fac.at[grp, source], fac.at[grp, source], fsend.at[o], frecv.at[o], (source, grp)).wait_recv()
+        fac_cross(o).start()
+        share(o, False).start()
+    for hop in far_hops:
+        stage(first, hop, False)
+        stage(first, hop, True)
+    stage(last, 0, True)
+    for o in range(n_pairs):
+        source = fac_source(o) + 1 - x
+        remote(fac.at[grp, source], fac.at[grp, source], gsend.at[o], grecv.at[o], (xmate, grp)).wait_recv()
+        share(o, True).start()
+    stage(last, 1, False)
+    stage(last, 1, True)
+    for far in (False, True):
+        for o in range(n_pairs):
+            source = fac_source(o) + (1 - x if far else x)
+            at = fac.at[other, source]
+            remote(at, at, psend.at[int(far), o], precv.at[int(far), o], (me, other)).wait_recv()
+    group = LANES // fac.shape[2]
+    for q in range(2):
+        for t in range(n_aux // group):
+            turned[q, :, t * LANES:(t + 1) * LANES] = fac[q, t * group:(t + 1) * group].reshape(LANES, -1).T
+    for n in first:
+        finish(n)
+    for hop in far_hops:
+        stage(last, hop, False)
+        stage(last, hop, True)
+    for n in last:
+        finish(n)
+
+    for n, dz, source, ways in sent:
+        def drain(n=n, source=source, ways=ways):
+            for way in ways:
+                when(edges[way], copy(n, source, way).wait_send)
+        when(valid(dz), drain)
+    for n in range(pieces):
+        for j in range(nj):
+            cross(n, j).wait_send()
+    half_copy().wait_send()
+    pairs_copy().wait_send()
+    for o in range(n_pairs):
+        if o:
+            fac_copy(o).wait_send()
+        fac_cross(o).wait_send()
+        share(o, False).wait_send()
+        share(o, True).wait_send()
+    for n in range(pieces):
+        for j in range(nj):
+            for rel, q in ((1, 0), (1, 1), (0, 1)):
+                give(n, rel, q, j).wait_send()
+                taken(n, rel, q, j).wait_recv()
+            give(n, 0, 0, j).wait()
+
+
+def panels(integrals, pairs, occupied, virtual, stored, n_aux, v):
+    depth = stored.shape[0]
+    aux_rows, nb, flat = integrals.shape
+    nocc = occupied.shape[0]
+    blk = math.isqrt(flat)
+    slab = virtual.shape[2]
+    nj = stored.shape[1] // v
+    piece = LANES
+    pieces = v // 4 // piece
+    cols = nocc * (slab // n_aux)
+    line = n_aux // PLANE
+    n_pairs = n_aux // 2
+    dma = pltpu.SemaphoreType.DMA
+    hbm = pl.BlockSpec(memory_space=pltpu.HBM)
+    return pl.pallas_call(
+        functools.partial(panel_kernel, n_aux, v, piece),
+        out_shape=jax.ShapeDtypeStruct((nj, cols, v), jnp.bfloat16),
+        in_specs=[hbm] * 5,
+        out_specs=hbm,
+        scratch_shapes=[
+            pltpu.VMEM((pieces, n_aux, depth, nj * piece), jnp.bfloat16),
+            pltpu.VMEM((2, n_aux, depth, 2 * cols), jnp.bfloat16),
+            pltpu.VMEM((2, 2 * cols, n_aux * depth), jnp.bfloat16),
+            pltpu.VMEM((pieces, 2, 2, cols, nj * piece), jnp.bfloat16),
+            pltpu.VMEM(integrals.shape, jnp.bfloat16),
+            pltpu.VMEM(virtual.shape, jnp.bfloat16),
+            pltpu.VMEM((nocc, nb, flat), jnp.float32),
+            pltpu.VMEM((nocc * aux_rows, nb, LANES), jnp.float32),
+            pltpu.VMEM((2, nocc * aux_rows, nb * blk), jnp.bfloat16),
+            pltpu.VMEM((n_pairs, depth, 2 * cols), jnp.bfloat16),
+            pltpu.VMEM((2, 2, nb), jnp.int32),
+            pltpu.SMEM((2, 2, nb), jnp.int32),
+            pltpu.VMEM(occupied.shape, jnp.bfloat16),
+            dma((4,)),
+            dma((pieces, nj)),
+            dma((pieces, nj)),
+            dma((pieces, nj)),
+            dma((pieces, 3, n_aux)),
+            dma((pieces, n_aux)),
+            dma((2,)),
+            dma((2,)),
+            dma((n_pairs,)),
+            dma((n_pairs,)),
+            dma((n_pairs,)),
+            dma((n_pairs,)),
+            dma((2, n_pairs)),
+            dma((2, n_pairs)),
+            dma((pieces, 4, nj)),
+            dma((pieces, 4, nj)),
+        ],
+        compiler_params=pltpu.CompilerParams(
+            collective_id=0, has_side_effects=True, vmem_limit_bytes=63 * 1024 * 1024),
+    )(integrals, pairs, occupied, virtual, stored)
+
+
 def make_per_device(n_aux, n_grp, v):
     def per_device(integrals, block_pairs, occupied, virtual, stored):
         nocc, nbas = occupied.shape
         local = virtual.shape[1] // n_aux
         blk = math.isqrt(integrals.shape[2])
+        if n_grp == 2 and n_aux % PLANE == 0 and v % (4 * LANES) == 0 and LANES % stored.shape[0] == 0:
+            panel = panels(integrals, block_pairs.transpose(0, 2, 1), occupied,
+                           virtual.reshape(nbas // blk, blk, -1), stored, n_aux, v)
+            return panel.transpose(1, 0, 2).reshape(nocc, local, panel.shape[0], v)
         occ = occupied.reshape(nocc, nbas // blk, blk)
-        panel = panels(integrals, block_pairs, occ, virtual, stored, n_aux, n_grp)
+        panel = panels_any(integrals, block_pairs, occ, virtual, stored, n_aux, n_grp)
         return panel.transpose(1, 0, 2).reshape(nocc, local, n_grp * panel.shape[2] // v, v)
 
     return per_device

time: 79.4 us -> 73.6 us (0.927)
  local copies, waits for them, and re-layouts: 8.27 us -> 5.5 us
  Pallas kernels: 69.5 us -> 67.1 us
    pallas_call x1, Pallas kernels: 69.5 us -> 67.1 us  [panels(): pl.pallas_call(functools.partial(panel_kernel, n_aux, v, piece), out_shap...]
    reshape x2 -> x1, local copies, waits for them, and re-layouts: 6.92 us -> 5.5 us  [per_device(): return panel.transpose(1, 0, 2).reshape(nocc, local, panel.shape[0], v)]
    unnamed x1 -> x0, local copies, waits for them, and re-layouts: 1.35 us -> none
where the time goes in v1:
time: 73.6 us; the launch traced here: 72.6 us
  Pallas kernels  67.1 us (91%)
  local copies, waits for them, and re-layouts  5.5 us (7%)
    pallas_call x1, Pallas kernels, panels(): pl.pallas_call(functools.partial(panel_kernel, n_aux, v, piece), out_shap...  67.1 us
    reshape x1, local copies, waits for them, and re-layouts, per_device(): return panel.transpose(1, 0, 2).reshape(nocc, local, panel.shape[0], v)  5.5 us

profile of v1, /device:TPU:5, one launch (start us, length us, event | category | flops | bytes accessed | tf_op | source)
XLA Modules:
  0.0 72.6 jit_solution(6342125751533433803)
XLA Ops:
  0.0 67.1 %shard_map.55 = bf16[2,192,3072]{2,1,0:T(8,128)(2,1)} custom-call(bf16[32,16,4096]{2,1,0:T(8,128)(2,1)} %integrals.1, s32[1,2,16]{2,1,0:T(2,128)} %bitcast.7, bf16[2,4096]{1,0:T(2,128)(2,1)} %occ_in.1, bf16[64,64,1536]{2,1,0:T(8,128)(2,1)} %bitcast.5, bf16[64,6144]{1,0:T(8,128)(2,1)} %stored.1), custom_call_target="tpu_custom_call" | custom-call | tf_op jit(solution)/shard_map/pallas_call | solution.py:681
  67.1 5.5 %copy.6 = bf16[2,96,2,3072]{3,2,1,0:T(2,128)(2,1)} copy(bf16[2,96,2,3072]{3,1,0,2:T(8,128)(2,1)} %bitcast.6) | data formatting | bytes 4718592 | tf_op jit(solution)/shard_map/reshape | solution.py:730

commit v2 on v1

--- a/solution.py
+++ b/solution.py
@@ -357,6 +357,28 @@
     )(integrals, pairs, occ, virtual, stored)
 
 
+HALVE, OWN, OTHER, FACTOR, CROSS, TURN, STORED, FINISH = range(8)
+JOINT = 0.67
+TUNED = (
+    (6, 1, 0, 0), (6, 3, 0, 0), (0,), (6, 5, 0, 0), (6, 1, 1, 0), (6, 0, 0, 0), (6, 2, 0, 1), (6, 3, 1, 0), (1,),
+    (6, 1, 2, 0), (6, 1, 0, 1), (6, 5, 0, 1), (6, 2, 0, 0), (6, 3, 0, 1), (6, 1, 3, 0), (6, 3, 2, 0), (2,),
+    (6, 2, 1, 0), (6, 5, 1, 1), (6, 1, 1, 1), (6, 3, 3, 0), (3, 0), (3, 2), (3, 3), (3, 5), (3, 4), (6, 3, 1, 1),
+    (4, 0), (6, 2, 2, 0), (3, 6), (4, 3), (6, 2, 3, 0), (6, 5, 1, 0), (3, 1), (3, 7), (6, 0, 0, 1), (4, 2),
+    (6, 1, 2, 1), (6, 2, 1, 1), (6, 1, 3, 1), (6, 5, 2, 0), (6, 3, 2, 1), (6, 5, 2, 1), (6, 4, 0, 0), (4, 5), (4, 1),
+    (6, 2, 2, 1), (6, 5, 3, 0), (4, 6), (4, 4), (6, 3, 3, 1), (6, 0, 1, 0), (6, 0, 1, 1), (6, 4, 0, 1), (4, 7),
+    (6, 5, 3, 1), (5,), (7, 1), (6, 0, 2, 0), (6, 0, 2, 1), (6, 4, 1, 1), (6, 0, 3, 0), (7, 3), (6, 2, 3, 1),
+    (6, 4, 1, 0), (6, 0, 3, 1), (6, 4, 2, 1), (7, 5), (7, 2), (6, 4, 2, 0), (6, 4, 3, 0), (6, 4, 3, 1), (7, 0),
+    (7, 4),
+)
+
+
+def plan(pieces, line, n_pairs):
+    stored = [(STORED, n, hop, far) for hop in range(line) for far in (0, 1) for n in range(pieces + 2)]
+    factor = [(kind, o) for kind in (FACTOR, CROSS) for o in range(n_pairs)]
+    plain = [(HALVE,), (OWN,), (OTHER,)] + stored + factor + [(TURN,)] + [(FINISH, n) for n in range(pieces + 2)]
+    return TUNED if sorted(TUNED) == sorted(plain) else plain
+
+
 def weigh_blocks(pairs, occ, weights):
     nocc, nbas = occ.shape
     nb = pairs.shape[1]
@@ -396,35 +418,38 @@
         half[grp, :, t * LANES:(t + 1) * LANES] = tile.astype(half.dtype)
 
 
-def expand(nocc, local, blk, index, half, virt, chunk):
+def expand(nocc, local, q, index, half, virt, chunk):
     n_grp, both, depth = half.shape
+    blk = virt.shape[1]
     aux_rows = both // nocc
     wide = 2 * local
     step = math.lcm(wide, 2 * LANES)
-    for q in range(n_grp):
-        for t in range(virt.shape[2] // step):
-            cols = slice(t * step, (t + 1) * step)
-            right = jnp.concatenate([virt[index[q, 1, k], :, cols] for k in range(depth // blk)], axis=0)
-            product = jnp.dot(half[q], right, preferred_element_type=jnp.float32).astype(chunk.dtype)
-            for c in range(step // wide):
-                for i in range(nocc):
-                    chunk[t * (step // wide) + c, q * aux_rows:(q + 1) * aux_rows, i * wide:(i + 1) * wide] = product[
-                        i * aux_rows:(i + 1) * aux_rows, c * wide:(c + 1) * wide]
-
-
-def panel_kernel(n_aux, v, piece, integrals, pairs_in, occ_in, virtual, stored, out, rows, fac, turned, block,
+    top = pl.ds(pl.multiple_of(q * aux_rows, aux_rows), aux_rows)
+    for t in range(virt.shape[2] // step):
+        cols = slice(t * step, (t + 1) * step)
+        right = jnp.concatenate([virt[index[q, 1, k], :, cols] for k in range(depth // blk)], axis=0)
+        product = jnp.dot(half[q], right, preferred_element_type=jnp.float32).astype(chunk.dtype)
+        for c in range(step // wide):
+            for i in range(nocc):
+                chunk[t * (step // wide) + c, top, i * wide:(i + 1) * wide] = product[
+                    i * aux_rows:(i + 1) * aux_rows, c * wide:(c + 1) * wide]
+
+
+def panel_kernel(n_aux, v, integrals, pairs_in, occ_in, virtual, stored, out, rows, wides, fac, turned, block, slab,
                  ints, virt, weights, part, half, chunk, pairs, index, occ,
-                 load_sem, own_sem, xsend, xrecv, send, recv, hsend, hrecv, fsend, frecv, gsend, grecv, psend, precv,
-                 osend, orecv):
+                 load_sem, own_sem, xsend, xrecv, send, recv, own_wide, xsend_wide, xrecv_wide, send_wide, recv_wide,
+                 hsend, hrecv, fsend, frecv, gsend, grecv, psend, precv, osend, orecv, wsend, wrecv):
     me = lax.axis_index("aux")
     grp = lax.axis_index("grp")
     other = 1 - grp
     line = n_aux // PLANE
     nj = stored.shape[1] // v
-    quarter = v // 4
-    pieces = quarter // piece
+    pieces = rows.shape[0]
+    piece = rows.shape[3] // nj
+    wide = wides.shape[3] // nj
+    base = 4 * pieces * piece
     nocc = occ.shape[0]
-    blk = math.isqrt(integrals.shape[2])
+    blk = virtual.shape[1]
     local = virtual.shape[2] // n_aux
     z = me // PLANE
     x = me % 2
@@ -433,25 +458,44 @@
     n_pairs = n_aux // 2
     xmate = me + 1 - 2 * x
     ymate = me + 2 * (1 - 2 * y)
-    targets = {"up": me + PLANE, "down": me - PLANE, "y": ymate}
-    slots = {"up": 0, "down": 1, "y": 2}
-    edges = {"up": z + 1 < line, "down": z >= 1, "y": None}
+    edges = {"up": z + 1 < line, "down": z >= 1, "x": None, "y": None}
+    targets = {"up": me + PLANE, "down": me - PLANE, "x": xmate, "y": ymate}
+    slots = {"up": 0, "down": 1, "x": 2, "y": 2}
     mine = 2 * x + grp
     theirs = 2 * (1 - x) + grp
 
     def column(j, q, n):
-        return pl.ds(pl.multiple_of(j * v + q * quarter + n * piece, LANES), piece)
+        return pl.ds(pl.multiple_of(j * v + (q * pieces + n) * piece, LANES), piece)
+
+    def column_wide(j, core, n):
+        return pl.ds(pl.multiple_of(j * v + base + (core * 2 + n) * wide, LANES), wide)
+
+    narrow = dict(
+        ref=rows, width=piece, own=own_sem, xsend=xsend, xrecv=xrecv, send=send, recv=recv, mate=xmate, last="y",
+        here=lambda j, n: column(j, mine, n), there=lambda j, n: column(j, theirs, n))
+    broad = [dict(
+        ref=wides, width=wide, own=own_wide, xsend=xsend_wide, xrecv=xrecv_wide, send=send_wide, recv=recv_wide,
+        mate=mate, last=last, here=lambda j, n: column_wide(j, grp, n), there=lambda j, n: column_wide(j, grp, n))
+        for mate, last in ((xmate, "y"), (ymate, "x"))]
+    every = [(narrow, n) for n in range(pieces)] + [(broad[n], n) for n in range(2)]
+
+    def at_of(kind, n, source, j):
+        return kind["ref"].at[n, source, :, pl.ds(j * kind["width"], kind["width"])]
+
+    def own_copy(kind, n, j):
+        return pltpu.make_async_copy(stored.at[:, kind["here"](j, n)], at_of(kind, n, me, j), kind["own"].at[n, j])
 
     load_pairs = pltpu.make_async_copy(pairs_in.at[0], pairs.at[grp], load_sem.at[0])
     load_pairs.start()
     load_occ = pltpu.make_async_copy(occ_in, occ, load_sem.at[1])
     load_occ.start()
+    load_index = pltpu.make_async_copy(pairs_in.at[0], index.at[grp], load_sem.at[4])
+    load_index.start()
     load_ints = pltpu.make_async_copy(integrals, ints, load_sem.at[2])
     load_ints.start()
-    for n in range(pieces):
+    for kind, n in every:
         for j in range(nj):
-            pltpu.make_async_copy(
-                stored.at[:, column(j, mine, n)], rows.at[n, me, :, pl.ds(j * piece, piece)], own_sem.at[n, j]).start()
+            own_copy(kind, n, j).start()
     load_virt = pltpu.make_async_copy(virtual, virt, load_sem.at[3])
     load_virt.start()
 
@@ -471,18 +515,19 @@
         return pltpu.make_async_remote_copy(
             src_ref=src, dst_ref=dst, send_sem=send_sem, recv_sem=recv_sem, device_id=device, device_id_type=MESH)
 
-    def copy(n, source, way):
-        at = rows.at[n, source]
-        return remote(at, at, send.at[n, slots[way], source], recv.at[n, source], (targets[way], grp))
-
-    def cross(n, j):
+    def copy(kind, n, source, way):
+        at = kind["ref"].at[n, source]
         return remote(
-            stored.at[:, column(j, theirs, n)], rows.at[n, me, :, pl.ds(j * piece, piece)],
-            xsend.at[n, j], xrecv.at[n, j], (xmate, grp))
-
-    def cross_wait(n, j):
-        at = rows.at[n, xmate, :, pl.ds(j * piece, piece)]
-        remote(at, at, xsend.at[n, j], xrecv.at[n, j], (xmate, grp)).wait_recv()
+            at, at, kind["send"].at[n, slots[way], source], kind["recv"].at[n, source], (targets[way], grp))
+
+    def cross(kind, n, j):
+        return remote(
+            stored.at[:, kind["there"](j, n)], at_of(kind, n, me, j),
+            kind["xsend"].at[n, j], kind["xrecv"].at[n, j], (kind["mate"], grp))
+
+    def cross_wait(kind, n, j):
+        at = at_of(kind, n, kind["mate"], j)
+        remote(at, at, kind["xsend"].at[n, j], kind["xrecv"].at[n, j], (kind["mate"], grp)).wait_recv()
 
     def valid(dz):
         if dz == 0:
@@ -491,30 +536,31 @@
 
     sent = []
 
-    def forward(n, dz, far):
-        source = (z - dz) * PLANE + y * 2 + (1 - x if far else x)
-        ways = ("up", "down", "y") if dz == 0 else (("up", "y") if dz > 0 else ("down", "y"))
-        sent.append((n, dz, source, ways))
+    def forward(kind, n, dz, far):
+        source = (kind["mate"] if far else me) - dz * PLANE
+        last = kind["last"]
+        ways = ("up", "down", last) if dz == 0 else (("up", last) if dz > 0 else ("down", last))
+        sent.append((kind, n, dz, source, ways))
 
         def act():
             if dz == 0:
                 for j in range(nj):
                     if far:
-                        cross_wait(n, j)
+                        cross_wait(kind, n, j)
                     else:
-                        at = rows.at[n, me, :, pl.ds(j * piece, piece)]
-                        pltpu.make_async_copy(stored.at[:, column(j, mine, n)], at, own_sem.at[n, j]).wait()
+                        own_copy(kind, n, j).wait()
             else:
-                copy(n, source, "y").wait_recv()
+                copy(kind, n, source, last).wait_recv()
             for way in ways:
-                when(edges[way], copy(n, source, way).start)
+                when(edges[way], copy(kind, n, source, way).start)
 
         when(valid(dz), act)
 
-    def stage(group, distance, far):
-        for n in group:
-            for dz in sorted({distance, -distance}):
-                forward(n, dz, far)
+    def stage(group, distance, *fars):
+        for kind, n in group:
+            for far in fars:
+                for dz in sorted({distance, -distance}):
+                    forward(kind, n, dz, far)
 
     def half_copy():
         return remote(half.at[grp], half.at[grp], hsend.at[0], hrecv.at[0], (me, other))
@@ -541,43 +587,118 @@
     def give(n, rel, q, j):
         to = (grp + q) % 2
         chip = 1 - x if rel else x
-        at = xmate if rel else me
-        src = block.at[n, to, chip, :, pl.ds(j * piece, piece)]
-        dst = out.at[j, :, column(0, mine, n)]
+        src = block.at[n, to, chip]
+        dst = out.at[:, :, column(0, mine, n)]
         if not rel and not q:
             return pltpu.make_async_copy(src, dst, osend.at[n, 0, j])
-        return remote(src, dst, osend.at[n, 2 * rel + q, j], orecv.at[n, 2 * rel + q, j], (at, to))
+        return remote(
+            src, dst, osend.at[n, 2 * rel + q, j], orecv.at[n, 2 * rel + q, j], (xmate if rel else me, to))
 
     def taken(n, rel, q, j):
         source = 2 * (1 - x if rel else x) + (grp + q) % 2
-        dst = out.at[j, :, column(0, source, n)]
-        src = block.at[n, 0, 0, :, pl.ds(j * piece, piece)]
-        return remote(src, dst, osend.at[n, 2 * rel + q, j], orecv.at[n, 2 * rel + q, j], (xmate, grp))
-
-    def finish(n):
+        return remote(
+            block.at[n, 0, 0], out.at[:, :, column(0, source, n)],
+            osend.at[n, 2 * rel + q, j], orecv.at[n, 2 * rel + q, j], (xmate, grp))
+
+    def pass_over(n, q, j):
+        to = (grp + q) % 2
+        src = slab.at[n, to]
+        dst = out.at[:, :, column_wide(0, grp, n)]
+        if not q:
+            return pltpu.make_async_copy(src, dst, wsend.at[n, q, j])
+        return remote(src, dst, wsend.at[n, q, j], wrecv.at[n, j], (me, to))
+
+    def passed(n, j):
+        return remote(
+            slab.at[n, 0], out.at[:, :, column_wide(0, other, n)],
+            wsend.at[n, 1, j], wrecv.at[n, j], (me, other))
+
+    def arrivals(kind, n):
+        mate = ymate if kind["last"] == "y" else xmate
         for dz in range(1 - line, line):
             for far in (0, 1):
-                source = (z - dz) * PLANE + (1 - y) * 2 + far
-
-                def arrive(source=source):
-                    copy(n, source, "y").wait_recv()
+                step = (kind["mate"] - me) if far else 0
+
+                def arrive(source=mate + step - dz * PLANE):
+                    copy(kind, n, source, kind["last"]).wait_recv()
 
                 when(valid(dz), arrive)
+
+    def finish(n):
+        arrivals(narrow, n)
         right = rows[n].reshape(-1, nj * piece)
         for q in range(2):
-            term = jnp.dot(turned[q], right, preferred_element_type=jnp.float32).astype(block.dtype)
-            for i in range(nocc):
-                for chip in range(2):
-                    top = (i * 2 + chip) * local
-                    block[n, q, chip, i * local:(i + 1) * local] = term[top:top + local]
+            left = turned[q].reshape(-1, right.shape[0])
+            term = jnp.dot(left, right, preferred_element_type=jnp.float32).astype(block.dtype)
+            for chip in range(2):
+                for j in range(nj):
+                    block[n, q, chip, :, j, :] = term[
+                        chip * nocc * local:(chip + 1) * nocc * local, j * piece:(j + 1) * piece]
         for rel, q in ((1, 0), (1, 1), (0, 1), (0, 0)):
-            for j in range(nj):
-                give(n, rel, q, j).start()
-
-    first = list(range((pieces + 1) // 2))
-    last = list(range((pieces + 1) // 2, pieces))
-    far_hops = range(2, line)
-
+            give(n, rel, q, 0).start()
+
+    def finish_wide(n):
+        arrivals(broad[n], n)
+        tile = math.gcd(2 * LANES, wide)
+        for q in (1, 0):
+            to = (grp + q) % 2
+            for t in range(nj * wide // tile):
+                cols = slice(t * tile, (t + 1) * tile)
+                right = wides[n, :, :, cols].reshape(-1, tile)
+                j, start = t * tile // wide, t * tile % wide
+                slab[n, to, :, j, start:start + tile] = jnp.dot(
+                    turned[to, x], right, preferred_element_type=jnp.float32).astype(slab.dtype)
+            pass_over(n, q, 0).start()
+
+    def wait_fac(o):
+        if o:
+            source = fac_source(o) + x
+            remote(fac.at[grp, source], fac.at[grp, source], fsend.at[o], frecv.at[o], (source, grp)).wait_recv()
+        else:
+            keep.wait()
+        fac_cross(o).start()
+        share(o, False).start()
+
+    def wait_cross(o):
+        source = fac_source(o) + 1 - x
+        remote(fac.at[grp, source], fac.at[grp, source], gsend.at[o], grecv.at[o], (xmate, grp)).wait_recv()
+        share(o, True).start()
+
+    def halve():
+        compact(blk, part, half, grp)
+        half_copy().start()
+
+    def expand_own():
+        load_index.wait()
+        load_virt.wait()
+        expand(nocc, local, grp, index, half, virt, chunk)
+
+    def expand_other():
+        remote(pairs.at[other], pairs.at[other], hsend.at[1], hrecv.at[1], (me, other)).wait_recv()
+        load_other = pltpu.make_async_copy(pairs.at[other], index.at[other], load_sem.at[0])
+        load_other.start()
+        load_other.wait()
+        remote(half.at[other], half.at[other], hsend.at[0], hrecv.at[0], (me, other)).wait_recv()
+        expand(nocc, local, other, index, half, virt, chunk)
+        for o in range(1, n_pairs):
+            fac_copy(o).start()
+        keep.start()
+
+    def turn():
+        for far in (False, True):
+            for o in range(n_pairs):
+                at = fac.at[other, fac_source(o) + (1 - x if far else x)]
+                remote(at, at, psend.at[int(far), o], precv.at[int(far), o], (me, other)).wait_recv()
+        group = LANES // fac.shape[2]
+        for q in range(2):
+            for t in range(n_aux // group):
+                tall = fac[q, t * group:(t + 1) * group].reshape(LANES, -1).T
+                for i in range(nocc):
+                    for chip in range(2):
+                        top = (i * 2 + chip) * local
+                        turned[q, chip, i * local:(i + 1) * local, t * LANES:(t + 1) * LANES] = tall[top:top + local]
+
+    keep = pltpu.make_async_copy(chunk.at[pair], fac.at[grp, me], load_sem.at[1])
     load_pairs.wait()
     load_occ.wait()
     weigh_blocks(pairs[grp], occ, weights)
@@ -585,69 +706,24 @@
     contract(blk, ints, weights, part)
     pl.semaphore_wait(barrier, len(peers))
     pairs_copy().start()
-    for n in range(pieces):
+    for kind, n in every:
         for j in range(nj):
-            cross(n, j).start()
-    stage(first, 0, False)
-    compact(blk, part, half, grp)
-    half_copy().start()
-    remote(pairs.at[other], pairs.at[other], hsend.at[1], hrecv.at[1], (me, other)).wait_recv()
-    load_index = pltpu.make_async_copy(pairs, index, load_sem.at[0])
-    load_index.start()
-    stage(first, 0, True)
-    load_index.wait()
-    load_virt.wait()
-    remote(half.at[other], half.at[other], hsend.at[0], hrecv.at[0], (me, other)).wait_recv()
-    expand(nocc, local, blk, index, half, virt, chunk)
-    for o in range(1, n_pairs):
-        fac_copy(o).start()
-    keep = pltpu.make_async_copy(chunk.at[pair], fac.at[grp, me], load_sem.at[1])
-    keep.start()
-    stage(first, 1, False)
-    stage(first, 1, True)
-    stage(last, 0, False)
-    keep.wait()
-    for o in range(n_pairs):
-        if o:
-            source = fac_source(o) + x
-            remote(fac.at[grp, source], fac.at[grp, source], fsend.at[o], frecv.at[o], (source, grp)).wait_recv()
-        fac_cross(o).start()
-        share(o, False).start()
-    for hop in far_hops:
-        stage(first, hop, False)
-        stage(first, hop, True)
-    stage(last, 0, True)
-    for o in range(n_pairs):
-        source = fac_source(o) + 1 - x
-        remote(fac.at[grp, source], fac.at[grp, source], gsend.at[o], grecv.at[o], (xmate, grp)).wait_recv()
-        share(o, True).start()
-    stage(last, 1, False)
-    stage(last, 1, True)
-    for far in (False, True):
-        for o in range(n_pairs):
-            source = fac_source(o) + (1 - x if far else x)
-            at = fac.at[other, source]
-            remote(at, at, psend.at[int(far), o], precv.at[int(far), o], (me, other)).wait_recv()
-    group = LANES // fac.shape[2]
-    for q in range(2):
-        for t in range(n_aux // group):
-            turned[q, :, t * LANES:(t + 1) * LANES] = fac[q, t * group:(t + 1) * group].reshape(LANES, -1).T
-    for n in first:
-        finish(n)
-    for hop in far_hops:
-        stage(last, hop, False)
-        stage(last, hop, True)
-    for n in last:
-        finish(n)
-
-    for n, dz, source, ways in sent:
-        def drain(n=n, source=source, ways=ways):
+            cross(kind, n, j).start()
+    steps = {
+        HALVE: halve, OWN: expand_own, OTHER: expand_other, FACTOR: wait_fac, CROSS: wait_cross, TURN: turn,
+        STORED: lambda n, hop, far: stage([every[n]], hop, far),
+        FINISH: lambda n: finish(n) if n < pieces else finish_wide(n - pieces)}
+    for step, *operands in plan(pieces, line, n_pairs):
+        steps[step](*operands)
+
+    for kind, n, dz, source, ways in sent:
+        def drain(kind=kind, n=n, source=source, ways=ways):
             for way in ways:
-                when(edges[way], copy(n, source, way).wait_send)
+                when(edges[way], copy(kind, n, source, way).wait_send)
         when(valid(dz), drain)
-    for n in range(pieces):
+    for kind, n in every:
         for j in range(nj):
-            cross(n, j).wait_send()
+            cross(kind, n, j).wait_send()
     half_copy().wait_send()
     pairs_copy().wait_send()
     for o in range(n_pairs):
@@ -657,11 +733,16 @@
         share(o, False).wait_send()
         share(o, True).wait_send()
     for n in range(pieces):
-        for j in range(nj):
+        for j in range(1):
             for rel, q in ((1, 0), (1, 1), (0, 1)):
                 give(n, rel, q, j).wait_send()
                 taken(n, rel, q, j).wait_recv()
             give(n, 0, 0, j).wait()
+    for n in range(2):
+        for j in range(1):
+            pass_over(n, 1, j).wait_send()
+            passed(n, j).wait_recv()
+            pass_over(n, 0, j).wait()
 
 
 def panels(integrals, pairs, occupied, virtual, stored, n_aux, v):
@@ -672,22 +753,24 @@
     slab = virtual.shape[2]
     nj = stored.shape[1] // v
     piece = LANES
-    pieces = v // 4 // piece
+    pieces = round(v // (4 * piece) * JOINT)
+    wide = (v - 4 * pieces * piece) // 4
     cols = nocc * (slab // n_aux)
-    line = n_aux // PLANE
     n_pairs = n_aux // 2
     dma = pltpu.SemaphoreType.DMA
     hbm = pl.BlockSpec(memory_space=pltpu.HBM)
     return pl.pallas_call(
-        functools.partial(panel_kernel, n_aux, v, piece),
-        out_shape=jax.ShapeDtypeStruct((nj, cols, v), jnp.bfloat16),
+        functools.partial(panel_kernel, n_aux, v),
+        out_shape=jax.ShapeDtypeStruct((cols, nj, v), jnp.bfloat16),
         in_specs=[hbm] * 5,
         out_specs=hbm,
         scratch_shapes=[
             pltpu.VMEM((pieces, n_aux, depth, nj * piece), jnp.bfloat16),
+            pltpu.VMEM((2, n_aux, depth, nj * wide), jnp.bfloat16),
             pltpu.VMEM((2, n_aux, depth, 2 * cols), jnp.bfloat16),
-            pltpu.VMEM((2, 2 * cols, n_aux * depth), jnp.bfloat16),
-            pltpu.VMEM((pieces, 2, 2, cols, nj * piece), jnp.bfloat16),
+            pltpu.VMEM((2, 2, cols, n_aux * depth), jnp.bfloat16),
+            pltpu.VMEM((pieces, 2, 2, cols, nj, piece), jnp.bfloat16),
+            pltpu.VMEM((2, 2, cols, nj, wide), jnp.bfloat16),
             pltpu.VMEM(integrals.shape, jnp.bfloat16),
             pltpu.VMEM(virtual.shape, jnp.bfloat16),
             pltpu.VMEM((nocc, nb, flat), jnp.float32),
@@ -697,12 +780,17 @@
             pltpu.VMEM((2, 2, nb), jnp.int32),
             pltpu.SMEM((2, 2, nb), jnp.int32),
             pltpu.VMEM(occupied.shape, jnp.bfloat16),
-            dma((4,)),
+            dma((5,)),
             dma((pieces, nj)),
             dma((pieces, nj)),
             dma((pieces, nj)),
             dma((pieces, 3, n_aux)),
             dma((pieces, n_aux)),
+            dma((2, nj)),
+            dma((2, nj)),
+            dma((2, nj)),
+            dma((2, 3, n_aux)),
+            dma((2, n_aux)),
             dma((2,)),
             dma((2,)),
             dma((n_pairs,)),
@@ -713,6 +801,8 @@
             dma((2, n_pairs)),
             dma((pieces, 4, nj)),
             dma((pieces, 4, nj)),
+            dma((2, 2, nj)),
+            dma((2, nj)),
         ],
         compiler_params=pltpu.CompilerParams(
             collective_id=0, has_side_effects=True, vmem_limit_bytes=63 * 1024 * 1024),
@@ -727,7 +817,7 @@
         if n_grp == 2 and n_aux % PLANE == 0 and v % (4 * LANES) == 0 and LANES % stored.shape[0] == 0:
             panel = panels(integrals, block_pairs.transpose(0, 2, 1), occupied,
                            virtual.reshape(nbas // blk, blk, -1), stored, n_aux, v)
-            return panel.transpose(1, 0, 2).reshape(nocc, local, panel.shape[0], v)
+            return panel.reshape(nocc, local, panel.shape[1], v)
         occ = occupied.reshape(nocc, nbas // blk, blk)
         panel = panels_any(integrals, block_pairs, occ, virtual, stored, n_aux, n_grp)
         return panel.transpose(1, 0, 2).reshape(nocc, local, n_grp * panel.shape[2] // v, v)

time: 73.6 us -> 71.5 us (0.971); the launches traced: 72.6 us -> 71.3 us
  local copies, waits for them, and re-layouts: 5.5 us -> 4.69 us
    reshape x1 -> x0, local copies, waits for them, and re-layouts: 5.5 us -> none  [per_device(): return panel.transpose(1, 0, 2).reshape(nocc, local, panel.shape[0], v)]
    unnamed x0 -> x1, local copies, waits for them, and re-layouts: none -> 4.69 us
where the time goes in v2:
time: 71.5 us; the launch traced here: 71.3 us
  Pallas kernels  66.7 us (93%)
  local copies, waits for them, and re-layouts  4.69 us (7%)
    pallas_call x1, Pallas kernels, panels(): pl.pallas_call(functools.partial(panel_kernel, n_aux, v), out_shape=jax.S...  66.7 us
    unnamed x1, local copies, waits for them, and re-layouts  4.69 us

profile of v2, /device:TPU:5, one launch (start us, length us, event | category | flops | bytes accessed | tf_op | source)
XLA Modules:
  0.0 71.3 jit_solution(7422809626386642715)
XLA Ops:
  0.0 66.7 %shard_map.55 = bf16[192,2,3072]{2,1,0:T(2,128)(2,1)} custom-call(bf16[32,16,4096]{2,1,0:T(8,128)(2,1)} %integrals.1, s32[1,2,16]{2,1,0:T(2,128)} %bitcast.5, bf16[2,4096]{1,0:T(2,128)(2,1)} %occ_in.1, bf16[64,64,1536]{2,1,0:T(8,128)(2,1)} %bitcast.3, bf16[64,6144]{1,0:T(8,128)(2,1)} %stored.1), custom_call_target="tpu_custom_call" | custom-call | tf_op jit(solution)/shard_map/pallas_call | solution.py:762
  66.7 4.7 %copy.7 = bf16[2,96,2,3072]{3,2,1,0:T(2,128)(2,1)} copy(bf16[2,96,2,3072]{3,2,1,0:T(2,128)(2,1)} %bitcast.4) | data formatting | bytes 4718592

commit v3 on v2

--- a/solution.py
+++ b/solution.py
@@ -407,6 +407,25 @@
                 picked, spread, preferred_element_type=jnp.float32)
 
 
+def contract_rows(blk, integrals, weights, part, low, high):
+    aux_rows = integrals.shape[0]
+    nocc = weights.shape[0]
+
+    @pl.loop(low, high)
+    def _(p):
+        for i in range(nocc):
+            sums = [None, None]
+            for t in range(integrals.shape[2] // LANES):
+                cols = slice(t * LANES, (t + 1) * LANES)
+                term = integrals[p, :, cols].astype(jnp.float32) * weights[i, :, cols]
+                sums[t % 2] = term if sums[t % 2] is None else sums[t % 2] + term
+            total = sums[0] + sums[1]
+            whole = total
+            for f in range(1, LANES // blk):
+                whole = whole + pltpu.roll(total, f * blk, 1)
+            part[i * aux_rows + p] = whole
+
+
 def compact(blk, part, half, grp):
     nb = part.shape[1]
     per = LANES // blk
@@ -450,6 +469,7 @@
     base = 4 * pieces * piece
     nocc = occ.shape[0]
     blk = virtual.shape[1]
+    aux_rows = integrals.shape[0]
     local = virtual.shape[2] // n_aux
     z = me // PLANE
     x = me % 2
@@ -665,6 +685,7 @@
         share(o, True).start()
 
     def halve():
+        contract_rows(blk, ints, weights, part, aux_rows // 2, aux_rows)
         compact(blk, part, half, grp)
         half_copy().start()
 
@@ -703,7 +724,7 @@
     load_occ.wait()
     weigh_blocks(pairs[grp], occ, weights)
     load_ints.wait()
-    contract(blk, ints, weights, part)
+    contract_rows(blk, ints, weights, part, 0, aux_rows // 2)
     pl.semaphore_wait(barrier, len(peers))
     pairs_copy().start()
     for kind, n in every:

time: 71.5 us -> 69.1 us (0.966)
  Pallas kernels: 66.7 us -> 64.2 us
    pallas_call x1, Pallas kernels: 66.7 us -> 64.2 us  [panels(): pl.pallas_call(functools.partial(panel_kernel, n_aux, v), out_shape=jax.S...]
where the time goes in v3:
time: 69.1 us; the launch traced here: 68.9 us
  Pallas kernels  64.2 us (93%)
  local copies, waits for them, and re-layouts  4.69 us (7%)
    pallas_call x1, Pallas kernels, panels(): pl.pallas_call(functools.partial(panel_kernel, n_aux, v), out_shape=jax.S...  64.2 us
    unnamed x1, local copies, waits for them, and re-layouts  4.69 us

profile of v3, /device:TPU:5, one launch (start us, length us, event | category | flops | bytes accessed | tf_op | source)
XLA Modules:
  0.0 68.9 jit_solution(11069631161068691539)
XLA Ops:
  0.0 64.2 %shard_map.55 = bf16[192,2,3072]{2,1,0:T(2,128)(2,1)} custom-call(bf16[32,16,4096]{2,1,0:T(8,128)(2,1)} %integrals.1, s32[1,2,16]{2,1,0:T(2,128)} %bitcast.5, bf16[2,4096]{1,0:T(2,128)(2,1)} %occ_in.1, bf16[64,64,1536]{2,1,0:T(8,128)(2,1)} %bitcast.3, bf16[64,6144]{1,0:T(8,128)(2,1)} %stored.1), custom_call_target="tpu_custom_call" | custom-call | tf_op jit(solution)/shard_map/pallas_call | solution.py:783
  64.2 4.7 %copy.7 = bf16[2,96,2,3072]{3,2,1,0:T(2,128)(2,1)} copy(bf16[2,96,2,3072]{3,2,1,0:T(2,128)(2,1)} %bitcast.4) | data formatting | bytes 4718592
